TPU v7x, 128 devices: a whole 4x4x4 slice. The times are simulated.
128 devices in a mesh: dp: 16 (over z, y_hi, core), tensor: 8 (over x, y_lo).
Axes of the slice: x: 4, y: 4 (y_hi: 2, y_lo: 2; y = y_hi * 2 + y_lo), z: 4, core: 2. Of those that a mesh axis runs over, the one named last changes fastest.
Arguments:
- train_states: bfloat16 [4096, 8192], P('dp'), may hold values from -6 to 6
- qkv_cotangent: bfloat16 [4096, 6144], P('dp', 'tensor'), may hold values from -0.09375 to 0.09375
- w_master: float32 [8192, 6144], P('dp', 'tensor'), may hold values from -1.1048543 to 1.1048543
- moment_one: float32 [8192, 6144], P('dp', 'tensor'), may hold values from -1.8 to 1.8
- moment_two: float32 [8192, 6144], P('dp', 'tensor'), may hold values from 0.02 to 2
- prompt_states: bfloat16 [8192, 8192], P('dp'), may hold values from -45 to 45
- norm_gain: float32 [8192], replicated, may hold values from 0.1 to 1.9
- w_out: bfloat16 [4096, 8192], P('tensor'), may hold values from -0.09375 to 0.09375
Outputs:
- update_dir: float32 [8192, 6144], P('dp', 'tensor')
- prefill_out: bfloat16 [8192, 8192], P(('dp', 'tensor'))
All inputs are finite; a program needn't handle non-finite values.
Results may differ from a plain program's by a relative error of at most 0.02.
Values may be sent and summed in bfloat16 or wider, within the bound.
A program may use at most 128 MiB of HBM per device.

v0:
```python
import jax
import jax.numpy as jnp
from jax import lax
from jax.sharding import PartitionSpec as P

HD = 128


beta_one = 0.9
beta_two = 0.95
bias_one = 1.0 - 0.9**8
bias_two = 1.0 - 0.95**8
learn_rate = 0.002
adam_eps = 1e-08
norm_eps = 1e-05
rope_base = 500000.0


def rope_tables(length, head_size):
    half_width = head_size // 2
    exponent = jnp.arange(half_width, dtype=jnp.float32) * (2.0 / head_size)
    inverse = jnp.power(jnp.float32(rope_base), -exponent)
    position = jnp.arange(length, dtype=jnp.float32)
    angles = position[:, None] * inverse[None, :]
    cosine_table = jnp.concatenate([jnp.cos(angles), jnp.cos(angles)], axis=1)
    sine_table = jnp.concatenate([jnp.sin(angles), jnp.sin(angles)], axis=1)
    return (cosine_table, sine_table)


def rotate(head_block, cosine_table, sine_table):
    half_width = head_block.shape[-1] // 2
    turned = jnp.concatenate([-head_block[..., half_width:], head_block[..., :half_width]], axis=-1)
    return head_block * cosine_table + turned * sine_table


def body(
    train_states, qkv_cotangent, w_master, moment_one, moment_two, prompt_states, norm_gain, w_out
):
    slice_width = w_master.shape[1]
    gradient = lax.psum_scatter(
        lax.dot_general(
            train_states,
            qkv_cotangent,
            (((0,), (0,)), ((), ())),
            preferred_element_type=jnp.float32,
        ).astype(jnp.bfloat16),
        "dp",
        scatter_dimension=0,
        tiled=True,
    ).astype(jnp.float32)
    moment_new = beta_one * moment_one + (1.0 - beta_one) * gradient
    second_new = beta_two * moment_two + (1.0 - beta_two) * gradient * gradient
    update_dir = moment_new / bias_one / (jnp.sqrt(second_new / bias_two) + adam_eps)
    owned_weight = (w_master - learn_rate * update_dir).astype(jnp.bfloat16)
    length = prompt_states.shape[0]
    widened = prompt_states.astype(jnp.float32)
    mean_square = jnp.mean(widened * widened, axis=1, keepdims=True)
    normed = (widened * lax.rsqrt(mean_square + norm_eps) * norm_gain).astype(jnp.bfloat16)
    projected = jnp.dot(
        normed,
        lax.all_gather(owned_weight, "dp", axis=0, tiled=True),
        preferred_element_type=jnp.float32,
    )
    query_width = slice_width - 2 * HD
    head_count = query_width // HD
    score_scale = HD ** (-0.5)
    cosine_table, sine_table = rope_tables(length, HD)
    queries = projected[:, :query_width].reshape(length, head_count, HD)
    queries = (
        rotate(queries, cosine_table[:, None, :], sine_table[:, None, :]) * score_scale
    ).astype(jnp.bfloat16)
    key_rows = rotate(
        projected[:, query_width : query_width + HD], cosine_table, sine_table
    ).astype(jnp.bfloat16)
    value_rows = projected[:, query_width + HD :].astype(jnp.bfloat16)
    scores = jnp.einsum("qhd,kd->hqk", queries, key_rows, preferred_element_type=jnp.float32)
    causal = jnp.arange(length)[:, None] >= jnp.arange(length)[None, :]
    scores = jnp.where(causal[None], scores, -jnp.inf)
    attend_weights = jax.nn.softmax(scores, axis=-1).astype(jnp.bfloat16)
    attended = jnp.einsum(
        "hqk,kd->qhd", attend_weights, value_rows, preferred_element_type=jnp.float32
    ).astype(jnp.bfloat16)
    attended = attended.reshape(length, query_width)
    summed = lax.psum_scatter(
        jnp.dot(attended, w_out, preferred_element_type=jnp.float32).astype(jnp.bfloat16),
        "tensor",
        scatter_dimension=0,
        tiled=True,
    )
    return (update_dir, summed)


def solution(mesh):
    placed = (
        P("dp", None),
        P("dp", "tensor"),
        P("dp", "tensor"),
        P("dp", "tensor"),
        P("dp", "tensor"),
        P("dp", None),
        P(),
        P("tensor", None),
    )
    return jax.shard_map(
        body,
        mesh=mesh,
        in_specs=placed,
        out_specs=(P("dp", "tensor"), P(("dp", "tensor"), None)),
        check_vma=False,
    )
```

profile of v0, /device:TPU:0, one launch (start us, length us, event | category | flops | bytes accessed | tf_op | source)
XLA Modules:
  0.0 435.2 jit_solution(55790417744570518)
XLA Ops:
  7.2 0.0 reduce-scatter.3.cloned.1.call-start
  7.2 0.9 copy-done
  8.2 10.2 %convolution_convert_fusion = bf16[8192,768]{1,0:T(8,128)(2,1)} fusion(bf16[256,8192]{1,0:T(8,128)(2,1)} %param.8, bf16[256,768]{1,0:T(8,128)(2,1)S(1)} %copy-done), kind=kOutput, calls=%fused_computation.6 | convolution fusion | flops 3227516928 | bytes 17170432 | tf_op jit(solution)/shard_map/dot_general | solution.py:41
  18.4 0.0 reduce-scatter.3.cloned.1.call-update
  18.4 0.0 all-gather.2.cloned.1.call-start
  18.5 125.0 %reduce-scatter.3.cloned.1.call-done = bf16[512,768]{1,0:T(8,128)(2,1)} async-done(((bf16[8192,768]{1,0:T(8,128)(2,1)}), bf16[512,768]{1,0:T(8,128)(2,1)}) %reduce-scatter.3.cloned.1.call-update) | async-done | bytes 786448 | tf_op jit(solution)/shard_map/reduce_scatter | solution.py:40
  143.5 4.2 subtract_convert_fusion
  147.8 0.0 all-gather.2.cloned.1.call-update
  147.8 0.2 reduce-scatter.5.cloned.1.call-start
  148.0 0.1 iota_compare_fusion
  148.1 1.0 fusion.31
  149.1 0.2 pad_maximum_fusion
  149.3 5.1 %fusion.1 = f32[512]{0:T(512)S(1)} fusion(bf16[512,8192]{1,0:T(8,128)(2,1)} %param.13), kind=kLoop, calls=%fused_computation.3 | loop fusion | flops 12582400 | bytes 8390656 | tf_op jit(solution)/shard_map/reduce_sum | solution.py:57
  154.5 82.6 %all-gather.2.cloned.1.call-done = bf16[8192,768]{1,0:T(8,128)(2,1)} async-done(((bf16[512,768]{1,0:T(8,128)(2,1)}), bf16[8192,768]{1,0:T(8,128)(2,1)}) %all-gather.2.cloned.1.call-update) | async-done | bytes 12582928 | tf_op jit(solution)/shard_map/all_gather | solution.py:61
  237.1 12.0 %fusion.4 = f32[512,768]{1,0:T(8,128)S(1)} fusion(bf16[8192,768]{1,0:T(8,128)(2,1)} %all-gather.2.cloned.1.call-done, bf16[512,8192]{1,0:T(8,128)(2,1)} %param.13, f32[8192]{0:T(1024)S(1)} %copy-done.4, f32[512]{0:T(512)S(1)} %add_rsqrt_fusion), kind=kOutput, calls=%fused_computation.8 | convolution fusion | flops 6459228160 | bytes 22579200 | tf_op jit(solution)/shard_map/dot_general | solution.py:59
  249.1 0.1 copy_bitcast_fusion
  249.2 0.1 slice_negate_fusion.1
  249.4 0.3 slice_negate_fusion
  249.7 0.9 fusion.23
  250.7 1.9 fusion.40
  252.6 0.5 fusion.19
  253.1 1.8 slice-done.1
  254.8 6.9 %convolution_convert_fusion.1 = bf16[512,8192]{1,0:T(8,128)(2,1)} fusion(bf16[512,512]{0,1:T(8,128)(2,1)S(1)} %bitcast.37, bf16[512,8192]{1,0:T(8,128)(2,1)S(1)} %bitcast.36), kind=kOutput, calls=%fused_computation.7 | convolution fusion | flops 4299161600 | bytes 17301504 | tf_op jit(solution)/shard_map/dot_general | solution.py:85
  261.7 166.9 %reduce-scatter.5.cloned.1.call-done = bf16[64,8192]{1,0:T(8,128)(2,1)} async-done(((bf16[512,8192]{1,0:T(8,128)(2,1)}), bf16[64,8192]{1,0:T(8,128)(2,1)}) %reduce-scatter.5.cloned.1.call-update) | async-done | bytes 1048592 | tf_op jit(solution)/shard_map/reduce_scatter | solution.py:84
  (16 shorter events, 0.1 us)
Async XLA Ops:
  7.2 1.0 copy-start
  7.2 136.3 %reduce-scatter.3.cloned.1.call-start = ((), (), s32[]{:S(2)}) async-start(), calls=%async_computation.2 | async-start | bytes 13369344 | tf_op jit(solution)/shard_map/reduce_scatter | solution.py:40
  18.4 125.1 %copy-start.2 = (f32[512,768]{1,0:T(8,128)S(1)}, f32[512,768]{1,0:T(8,128)}, u32[]{:S(2)}) copy-start(f32[512,768]{1,0:T(8,128)} %param.10) | copy-start | bytes 4718596
  18.4 125.1 %copy-start.3 = (f32[512,768]{1,0:T(8,128)S(1)}, f32[512,768]{1,0:T(8,128)}, u32[]{:S(2)}) copy-start(f32[512,768]{1,0:T(8,128)} %param.12) | copy-start | bytes 4718596
  18.4 218.6 %all-gather.2.cloned.1.call-start = ((), (), s32[]{:S(2)}) async-start(), calls=%async_computation.3 | async-start | bytes 13369344 | tf_op jit(solution)/shard_map/all_gather | solution.py:61
  147.8 280.8 %reduce-scatter.5.cloned.1.call-start = ((), (), s32[]{:S(2)}) async-start(), calls=%async_computation.4 | async-start | bytes 9437184 | tf_op jit(solution)/shard_map/reduce_scatter | solution.py:84
  149.3 87.8 %copy-start.4 = (f32[8192]{0:T(1024)S(1)}, f32[8192]{0:T(1024)}, u32[]{:S(2)}) copy-start(f32[8192]{0:T(1024)} %param.14) | copy-start | bytes 98308
  250.6 2.4 slice-start
  252.6 2.3 slice-start.1
  261.7 167.0 %copy-start.1 = (bf16[256,768]{1,0:T(8,128)(2,1)S(1)}, bf16[256,768]{1,0:T(8,128)(2,1)}, u32[]{:S(2)}) copy-start(bf16[256,768]{1,0:T(8,128)(2,1)} %param.9) | copy-start | bytes 1179652
Sparse Core Ops, SparseCore 0:
  18.6 124.9 reduce-scatter.2
  147.9 89.1 all-gather.1
  261.8 166.7 reduce-scatter.4
where the time goes:
time: 436 us; the launch traced here: 435 us
  waiting for transfers between devices  375 us (86%)
  matrix products  30.5 us (7%)
  between operations  13.9 us (3%)
  other arithmetic  13 us (3%)
    reduce_scatter x1, waiting for transfers between devices, body(): lax.psum_scatter(jnp.dot(attended, w_out, preferred_element_type=jnp.floa...  167 us
    reduce_scatter x1, waiting for transfers between devices, body(): lax.psum_scatter(lax.dot_general(train_states, qkv_cotangent, (((0,), (0,...  125 us
    all_gather x1, waiting for transfers between devices, body(): lax.all_gather(owned_weight, 'dp', axis=0, tiled=True)  82.6 us
    dot_general x1, matrix products, body(): jnp.dot(normed, lax.all_gather(owned_weight, 'dp', axis=0, tiled=True), p...  12 us
    dot_general x1, matrix products, body(): lax.dot_general(train_states, qkv_cotangent, (((0,), (0,)), ((), ())), pr...  10.2 us
  transfers between devices with their start and end apart: 3, of which 3 were waited for; matrix products, arithmetic and copies ran while one was open for 1% of the time, Pallas kernels for 0%

commit v1 on v0

v1 whole, which is shorter than its diff:
```python
import functools

import jax
import jax.numpy as jnp
import numpy as np
from jax import lax
from jax.experimental import pallas as pl
from jax.experimental.pallas import tpu as pltpu
from jax.sharding import PartitionSpec as P

HD = 128
QH = 4
LEN = 512
D = 8192
N_DP = 16
N_T = 8
SLICE = (QH + 2) * HD
QW = QH * HD
ROWS = D // N_DP
TOK = 256
SUB = TOK // N_T
HALF = D // 2
CHUNKS = 4
CW = HALF // CHUNKS

beta_one = 0.9
beta_two = 0.95
bias_one = 1.0 - 0.9**8
bias_two = 1.0 - 0.95**8
learn_rate = 0.002
adam_eps = 1e-08
norm_eps = 1e-05
rope_base = 500000.0

MESH = pl.DeviceIdType.MESH
BF = jnp.bfloat16
F32 = jnp.float32


def place():
    d = lax.axis_index("dp")
    t = lax.axis_index("tensor")
    return d, t, d // 4, (d // 2) % 2, d % 2, t // 2, t % 2


def mo(v, m):
    return pl.multiple_of(v, m)


def greet(peers):
    barrier = pltpu.get_barrier_semaphore()
    for peer in peers:
        pl.semaphore_signal(barrier, inc=1, device_id=peer, device_id_type=MESH)
    pl.semaphore_wait(barrier, len(peers))


class Copies:
    def __init__(self, send, recv):
        self.send, self.recv, self.made, self.used = send, recv, {}, 0

    def start(self, name, src, dst, peer):
        cp = pltpu.make_async_remote_copy(
            src_ref=src,
            dst_ref=dst,
            send_sem=self.send.at[self.used],
            recv_sem=self.recv.at[self.used],
            device_id=peer,
            device_id_type=MESH,
        )
        self.used += 1
        self.made[name] = cp
        cp.start()

    def arrived(self, *names):
        for name in names:
            self.made[name].wait_recv()

    def drain(self):
        for cp in self.made.values():
            cp.wait_send()


class Gather:
    def __init__(self, tag, cps, buf, index, rows, cross, nxt, prv, partner, core=None):
        self.tag, self.cps, self.buf, self.index = tag, cps, buf, index
        self.rows, self.cross = rows, cross
        self.nxt, self.prv, self.partner, self.core = nxt, prv, partner, core

    def piece(self, rr, plane, lo, hi):
        return self.buf.at[self.index(rr, plane), pl.ds(lo, hi - lo), :]

    def go(self, name, rr, plane, lo, hi, peer, src=None):
        dst = self.piece(rr, plane, lo, hi)
        if src is None:
            src = dst
        self.cps.start(self.tag + name, src, dst, peer)

    def wait(self, *names):
        self.cps.arrived(*[self.tag + name for name in names])

    def begin(self, own=None):
        rows, cross = self.rows, self.cross
        half, ch = rows // 2, self.cross // 2

        def src(lo, hi):
            if own is None:
                return None
            return own.at[pl.ds(lo, hi - lo), :]

        def send(name, lo, hi, peer):
            self.go(name, 0, 0, lo, hi, peer, src(lo, hi))

        send("oA+", 0, half, self.nxt)
        send("oB-", half, rows, self.prv)
        send("oPA", 0, ch, self.partner)
        send("oPB", ch, cross, self.partner)
        send("oB+", half, rows, self.nxt)
        send("oA-", 0, half, self.prv)
        if cross < rows:
            send("oP2", cross, rows, self.partner)
        if self.core is not None:
            send("c00", 0, rows, self.core)

    def step1(self):
        half, rows = self.rows // 2, self.rows
        self.wait("oA+")
        self.go("fA+", -1, 0, 0, half, self.nxt)
        self.wait("oB-")
        self.go("fB-", 1, 0, half, rows, self.prv)

    def step2(self):
        cross, ch = self.cross, self.cross // 2
        self.wait("oPA")
        self.go("pA+", 0, 1, 0, ch, self.nxt)
        self.wait("oPB")
        self.go("pB-", 0, 1, ch, cross, self.prv)
        self.go("pB+", 0, 1, ch, cross, self.nxt)
        self.go("pA-", 0, 1, 0, ch, self.prv)
        if cross < self.rows:
            self.wait("oP2")
        if self.core is not None:
            self.go("c01", 0, 1, 0, self.rows, self.core)

    def step3(self):
        rows, cross = self.rows, self.cross
        self.wait("oB+", "oA-")
        if cross < rows:
            self.go("y-", -1, 0, cross, rows, self.partner)
            self.go("y+", 1, 0, cross, rows, self.partner)
        if self.core is not None:
            self.go("c-0", -1, 0, 0, rows, self.core)
            self.go("c+0", 1, 0, 0, rows, self.core)

    def step4(self):
        rows, cross = self.rows, self.cross
        self.wait("fA+", "fB-")
        if cross < rows:
            self.go("y2", 2, 0, cross, rows, self.partner)
        if self.core is not None:
            self.go("c20", 2, 0, 0, rows, self.core)

    def step5(self):
        cross, ch = self.cross, self.cross // 2
        self.wait("pA+")
        self.go("qA+", -1, 1, 0, ch, self.nxt)
        self.wait("pB-")
        self.go("qB-", 1, 1, ch, cross, self.prv)

    def step6(self):
        self.wait("pB+", "pA-")
        if self.cross < self.rows:
            self.wait("y-", "y+")
        if self.core is not None:
            self.go("c-1", -1, 1, 0, self.rows, self.core)
            self.go("c+1", 1, 1, 0, self.rows, self.core)

    def step7(self):
        self.wait("qA+", "qB-")
        if self.cross < self.rows:
            self.wait("y2")
        if self.core is not None:
            self.go("c21", 2, 1, 0, self.rows, self.core)


def dp_of(z, yh, c):
    return lax.rem(z + 4, 4) * 4 + yh * 2 + c


def t_of(x, yl):
    return lax.rem(x + 4, 4) * 2 + yl


def grad_kernel(
    s_ref, c_ref, w_ref, m1_ref, m2_ref, upd_ref, new_ref,
    sb, cb, g, wv, m1v, m2v, send, recv, local,
):
    d, t, z, yh, c, x, yl = place()
    core = (d + 1 - 2 * c, t)
    yhp = (dp_of(z, 1 - yh, c), t)
    ylp = (d, t_of(x, 1 - yl))
    xn, xp = (d, t_of(x + 1, yl)), (d, t_of(x - 1, yl))
    zn, zp = (dp_of(z + 1, yh, c), t), (dp_of(z - 1, yh, c), t)
    others = [lax.rem(d + j, N_DP) for j in range(1, N_DP)]

    loads = [
        pltpu.make_async_copy(c_ref, cb.at[d], local.at[0]),
        pltpu.make_async_copy(
            s_ref.at[pl.ds(mo(t * SUB, SUB), SUB), pl.ds(mo(d * ROWS, ROWS), ROWS)],
            sb.at[t, pl.ds(mo(d * SUB, SUB), SUB), :],
            local.at[1],
        ),
        pltpu.make_async_copy(w_ref, wv, local.at[2]),
        pltpu.make_async_copy(m1_ref, m1v, local.at[3]),
        pltpu.make_async_copy(m2_ref, m2v, local.at[4]),
    ]
    for cp in loads:
        cp.start()
    greet([(e, t) for e in others] + [xn, xp, ylp])

    cps = Copies(send, recv)
    for j, e in enumerate(others):
        cps.start(
            ("a", j),
            s_ref.at[pl.ds(mo(t * SUB, SUB), SUB), pl.ds(mo(e * ROWS, ROWS), ROWS)],
            sb.at[t, pl.ds(mo(d * SUB, SUB), SUB), :],
            (e, t),
        )
    cot = Gather(
        "c", cps, cb, lambda rr, p: dp_of(z + rr, yh + p * (1 - 2 * yh), c),
        TOK, CROSS_C, zn, zp, yhp, core,
    )
    sta = Gather(
        "s", cps, sb, lambda rr, p: t_of(x + rr, yl + p * (1 - 2 * yl)),
        N_DP * SUB, CROSS_S, xn, xp, ylp,
    )
    cot.begin(c_ref)
    cps.arrived(*[("a", j) for j in range(N_DP - 1)])
    loads[1].wait()
    sta.begin()
    cot.step1()
    cot.step2()
    sta.step1()
    cot.step3()
    sta.step2()
    cot.step4()
    cot.step5()
    sta.step3()
    sta.step4()
    cot.step6()
    cot.step7()
    sta.step5()
    loads[0].wait()
    cps.arrived(*["c" + n for n in ("c00", "c01", "c-0", "c+0", "c20", "c-1", "c+1", "c21")])

    def term(tb):
        cc = cb[:, pl.ds(mo(tb * SUB, SUB), SUB), :].reshape(N_DP * SUB, SLICE)
        return lax.dot_general(
            sb[tb], cc, (((0,), (0,)), ((), ())), preferred_element_type=F32
        )

    g[...] = term(t)

    def ring(plane):
        def one(i, carry):
            g[...] += term(sta.index(i, plane))
            return carry

        return one

    lax.fori_loop(1, 4, ring(0), 0)
    g[...] += term(sta.index(0, 1))
    sta.step6()
    sta.step7()
    lax.fori_loop(1, 4, ring(1), 0)
    for cp in loads[2:]:
        cp.wait()

    def adam(i, carry):
        r = pl.ds(mo(i * 32, 32), 32)
        grad = g[r, :]
        moment = beta_one * m1v[r, :] + (1.0 - beta_one) * grad
        second = beta_two * m2v[r, :] + (1.0 - beta_two) * grad * grad
        upd = moment / bias_one / (jnp.sqrt(second / bias_two) + adam_eps)
        upd_ref[r, :] = upd
        new_ref[r, :] = (wv[r, :] - learn_rate * upd).astype(BF)
        return carry

    lax.fori_loop(0, ROWS // 32, adam, 0)
    cps.drain()


def block_kernel(
    new_ref, x_ref, gain_ref, wo_ref, cos_ref, sin_ref, out_ref,
    wb, nb, stage, acc, kv, att, woo, wop, part, r1, r2, fp,
    send, recv, send2, recv2, local,
):
    d, t, z, yh, c, x, yl = place()
    core = (d + 1 - 2 * c, t)
    yhp = (dp_of(z, 1 - yh, c), t)
    ylp = (d, t_of(x, 1 - yl))
    xn, xp = (d, t_of(x + 1, yl)), (d, t_of(x - 1, yl))
    zn, zp = (dp_of(z + 1, yh, c), t), (dp_of(z - 1, yh, c), t)
    mine = mo(yl * HALF, HALF)
    theirs = mo((1 - yl) * HALF, HALF)
    NR = 64

    def fetch(i):
        return pltpu.make_async_copy(
            x_ref.at[pl.ds(mo(i * NR, NR), NR), :], stage.at[lax.rem(i, 2)],
            local.at[lax.rem(i, 2)],
        )

    own = pltpu.make_async_copy(new_ref, wb.at[d], local.at[2])
    out_w = pltpu.make_async_copy(wo_ref.at[:, pl.ds(mine, HALF)], woo, local.at[3])
    fetch(0).start()
    own.start()
    greet([core, yhp, ylp, xn, xp, zn, zp])

    cps = Copies(send, recv)
    gat = Gather(
        "w", cps, wb, lambda rr, p: dp_of(z + rr, yh + p * (1 - 2 * yh), c),
        ROWS, CROSS_W, zn, zp, yhp, core,
    )
    gat.begin(new_ref)
    wrows = pl.ds(mo(c * (QW // 2), QW // 2), QW // 2)
    cps.start("wo", wo_ref.at[wrows, pl.ds(theirs, HALF)], wop.at[wrows, :], ylp)

    def norm(i, carry):
        @pl.when(i + 1 < LEN // NR)
        def _():
            fetch(i + 1).start()

        fetch(i).wait()
        slot = lax.rem(i, 2)

        def rows16(k, carry):
            r = pl.ds(mo(k * 16, 16), 16)
            ro = pl.ds(mo(i * NR + k * 16, 16), 16)
            tot = jnp.zeros((16, ROWS), F32)
            for j in range(N_DP):
                v = stage[slot, r, j * ROWS : (j + 1) * ROWS].astype(F32)
                tot = tot + v * v
            scale = lax.rsqrt(jnp.sum(tot, axis=1, keepdims=True) * (1.0 / D) + norm_eps)
            for j in range(N_DP):
                v = stage[slot, r, j * ROWS : (j + 1) * ROWS].astype(F32)
                gj = gain_ref[:, j * ROWS : (j + 1) * ROWS]
                nb[j, ro, :] = (v * scale * gj).astype(BF)
            return carry

        lax.fori_loop(0, NR // 16, rows16, 0)
        return carry

    lax.fori_loop(0, LEN // NR, norm, 0)
    out_w.start()

    def term(e):
        return jnp.dot(nb[e], wb[e], preferred_element_type=F32)

    def pair(rr, plane):
        base = dp_of(z + rr, yh + plane * (1 - 2 * yh), 0)

        def one(i, carry):
            acc[...] += term(base + i)
            return carry

        lax.fori_loop(0, 2, one, 0)

    own.wait()
    gat.step1()
    gat.step2()
    acc[...] = term(d)
    cps.arrived("wc00")
    acc[...] += term(d + 1 - 2 * c)
    gat.step3()
    gat.step4()
    cps.arrived("wc01")
    pair(0, 1)
    gat.step5()
    cps.arrived("wc-0", "wc+0", "wc20")

    def ring(plane):
        def one(i, carry):
            e = dp_of(z + 1 + i // 2, yh + plane * (1 - 2 * yh), lax.rem(i, 2))
            acc[...] += term(e)
            return carry

        lax.fori_loop(0, 6, one, 0)

    ring(0)
    cps.arrived("wo")
    cps.start("woc", wop.at[wrows, :], wop.at[wrows, :], core)
    gat.step6()
    gat.step7()
    cps.arrived("wc-1", "wc+1", "wc21")
    ring(1)

    def rope(u):
        return u * cos_ref[...] + pltpu.roll(u, HD // 2, 1) * sin_ref[...]

    kv[0] = rope(acc[:, QW : QW + HD]).astype(BF)
    kv[1] = acc[:, QW + HD :].astype(BF)
    HL = LEN // 2
    for h in range(QH):
        cols = slice(h * HD, (h + 1) * HD)
        q = (rope(acc[:, cols]) * (HD**-0.5)).astype(BF)
        for b in range(2):
            n = HL * (b + 1)
            s = lax.dot_general(
                q[b * HL : n], kv[0, :n], (((1,), (1,)), ((), ())),
                preferred_element_type=F32,
            )
            qi = lax.broadcasted_iota(jnp.int32, (HL, n), 0) + b * HL
            ki = lax.broadcasted_iota(jnp.int32, (HL, n), 1)
            s = jnp.where(qi >= ki, s, -jnp.inf)
            e = jnp.exp(s - jnp.max(s, axis=1, keepdims=True))
            a = (e / jnp.sum(e, axis=1, keepdims=True)).astype(BF)
            att[0, b * HL : n, cols] = jnp.dot(
                a, kv[1, :n], preferred_element_type=F32
            ).astype(BF)
        cps.start(("at", h), att.at[0, :, cols], att.at[1, :, cols], ylp)

    out_w.wait()
    cps.arrived("woc")
    cps.arrived(*[("at", h) for h in range(QH)])

    XB = LEN // 4
    HC = CW // 2

    def rows_of(xx):
        return pl.ds(mo(lax.rem(xx + 4, 4) * XB, XB), XB)

    def cols_of(k, w=CW, off=0):
        return pl.ds(mo(k * CW + off, HC), w)

    def remote(src, dst, i, peer):
        return pltpu.make_async_remote_copy(
            src_ref=src, dst_ref=dst, send_sem=send2.at[i], recv_sem=recv2.at[i],
            device_id=peer, device_id_type=MESH,
        )

    def far(k):
        hc = pl.ds(mo(k * HC, HC), HC)
        return (
            remote(part.at[rows_of(x + 2), cols_of(k, HC)], r1.at[0, :, hc], k, xn),
            remote(part.at[rows_of(x + 2), cols_of(k, HC, HC)], r1.at[1, :, hc], CHUNKS + k, xp),
        )

    def near(k):
        return (
            remote(part.at[rows_of(x + 1), cols_of(k)], r2.at[0, :, cols_of(k)], 2 * CHUNKS + k, xn),
            remote(part.at[rows_of(x - 1), cols_of(k)], r2.at[1, :, cols_of(k)], 3 * CHUNKS + k, xp),
        )

    def last(k):
        oc = pl.ds(mo(mine + k * CW, CW), CW)
        return remote(fp.at[:, cols_of(k)], out_ref.at[:, oc], 4 * CHUNKS + k, ylp)

    def produce(k, carry):
        def tile(j, carry):
            cc = pl.ds(mo(k * CW + j * 256, 256), 256)
            part[:, cc] = (
                jnp.dot(att[0], woo[:, cc], preferred_element_type=F32)
                + jnp.dot(att[1], wop[:, cc], preferred_element_type=F32)
            ).astype(BF)
            return carry

        lax.fori_loop(0, CW // 256, tile, 0)
        for cp in far(k):
            cp.start()
        return carry

    def forward(k, carry):
        hc = pl.ds(mo(k * HC, HC), HC)
        up, down = far(k)
        to_next, to_prev = near(k)
        for i, (cp, nx, rows, cc) in enumerate(
            (
                (up, to_next, rows_of(x + 1), cols_of(k, HC)),
                (down, to_prev, rows_of(x - 1), cols_of(k, HC, HC)),
            )
        ):
            cp.wait_recv()
            part[rows, cc] = (part[rows, cc].astype(F32) + r1[i, :, hc].astype(F32)).astype(BF)
            nx.start()
        return carry

    def finish(k, carry):
        to_next, to_prev = near(k)
        to_next.wait_recv()
        to_prev.wait_recv()
        SR = LEN // N_T

        def total(half):
            rows = pl.ds(mo(x * XB + half * SR, SR), SR)
            rr = pl.ds(mo(half * SR, SR), SR)
            cc = cols_of(k)
            return (
                part[rows, cc].astype(F32)
                + r2[0, rr, cc].astype(F32)
                + r2[1, rr, cc].astype(F32)
            ).astype(BF)

        fp[:, cols_of(k)] = total(1 - yl)
        last(k).start()
        out_ref[:, pl.ds(mo(mine + k * CW, CW), CW)] = total(yl)
        return carry

    def close(k, carry):
        for cp in far(k) + near(k):
            cp.wait_send()
        last(k).wait()
        return carry

    lax.fori_loop(0, CHUNKS, produce, 0)
    lax.fori_loop(0, CHUNKS, forward, 0)
    lax.fori_loop(0, CHUNKS, finish, 0)
    lax.fori_loop(0, CHUNKS, close, 0)
    cps.drain()


CROSS_C = TOK
CROSS_S = N_DP * SUB
CROSS_W = ROWS


def tables():
    half = HD // 2
    exponent = np.arange(half, dtype=np.float32) * np.float32(2.0 / HD)
    inverse = np.power(np.float64(rope_base), -exponent.astype(np.float64)).astype(np.float32)
    angles = np.arange(LEN, dtype=np.float32)[:, None] * inverse[None, :]
    cos = np.cos(angles.astype(np.float64)).astype(np.float32)
    sin = np.sin(angles.astype(np.float64)).astype(np.float32)
    return np.concatenate([cos, cos], 1), np.concatenate([-sin, sin], 1)


ANY = pl.BlockSpec(memory_space=pl.ANY)
VM = pl.BlockSpec(memory_space=pltpu.VMEM)


def body(
    train_states, qkv_cotangent, w_master, moment_one, moment_two, prompt_states, norm_gain, w_out
):
    dma = pltpu.SemaphoreType.DMA
    update_dir, fresh = pl.pallas_call(
        grad_kernel,
        name="grad_adam",
        out_shape=(
            jax.ShapeDtypeStruct((ROWS, SLICE), F32),
            jax.ShapeDtypeStruct((ROWS, SLICE), BF),
        ),
        in_specs=[ANY] * 5,
        out_specs=(VM, VM),
        scratch_shapes=[
            pltpu.VMEM((N_T, N_DP * SUB, ROWS), BF),
            pltpu.VMEM((N_DP, TOK, SLICE), BF),
            pltpu.VMEM((ROWS, SLICE), F32),
            pltpu.VMEM((ROWS, SLICE), F32),
            pltpu.VMEM((ROWS, SLICE), F32),
            pltpu.VMEM((ROWS, SLICE), F32),
            dma((64,)),
            dma((64,)),
            dma((5,)),
        ],
        compiler_params=pltpu.CompilerParams(
            collective_id=1, has_side_effects=True, vmem_limit_bytes=60 << 20
        ),
    )(train_states, qkv_cotangent, w_master, moment_one, moment_two)
    cos, sin = tables()
    out = pl.pallas_call(
        block_kernel,
        name="prefill",
        out_shape=jax.ShapeDtypeStruct((LEN // N_T, D), BF),
        in_specs=[ANY, ANY, VM, ANY, VM, VM],
        out_specs=VM,
        scratch_shapes=[
            pltpu.VMEM((N_DP, ROWS, SLICE), BF),
            pltpu.VMEM((N_DP, LEN, ROWS), BF),
            pltpu.VMEM((2, 64, D), BF),
            pltpu.VMEM((LEN, SLICE), F32),
            pltpu.VMEM((2, LEN, HD), BF),
            pltpu.VMEM((2, LEN, QW), BF),
            pltpu.VMEM((QW, HALF), BF),
            pltpu.VMEM((QW, HALF), BF),
            pltpu.VMEM((LEN, HALF), BF),
            pltpu.VMEM((2, LEN // 4, HALF // 2), BF),
            pltpu.VMEM((2, LEN // 4, HALF), BF),
            pltpu.VMEM((LEN // N_T, HALF), BF),
            dma((48,)),
            dma((48,)),
            dma((5 * CHUNKS,)),
            dma((5 * CHUNKS,)),
            dma((4,)),
        ],
        compiler_params=pltpu.CompilerParams(
            collective_id=2, has_side_effects=True, vmem_limit_bytes=63 << 20
        ),
    )(fresh, prompt_states, norm_gain.reshape(1, D), w_out, jnp.asarray(cos), jnp.asarray(sin))
    return (update_dir, out)


def solution(mesh):
    placed = (
        P("dp", None),
        P("dp", "tensor"),
        P("dp", "tensor"),
        P("dp", "tensor"),
        P("dp", "tensor"),
        P("dp", None),
        P(),
        P("tensor", None),
    )
    return jax.shard_map(
        body,
        mesh=mesh,
        in_specs=placed,
        out_specs=(P("dp", "tensor"), P(("dp", "tensor"), None)),
        check_vma=False,
    )
```

time: 436 us -> 198 us (0.45)
  waiting for transfers between devices: 375 us -> 0 us
  Pallas kernels: 0 us -> 193 us
  matrix products: 30.5 us -> 0 us
  between operations: 13.9 us -> 0.66 us
  other arithmetic: 13 us -> 0 us
    reduce_scatter x2 -> x0, waiting for transfers between devices: 292 us -> none  [the longest x1 167 us: body(): lax.psum_scatter(jnp.dot(attended, w_out, preferred_element_type=jnp.floa...]
    pallas_call x0 -> x2, Pallas kernels: none -> 193 us  [the longest x1 134 us: body(): pl.pallas_call(block_kernel, name='prefill', out_shape=jax.ShapeDtypeStru...]
    all_gather x1 -> x0, waiting for transfers between devices: 82.6 us -> none  [body(): lax.all_gather(owned_weight, 'dp', axis=0, tiled=True)]
    dot_general x5 -> x0, matrix products: 30.5 us -> none  [the longest x1 12 us: body(): jnp.dot(normed, lax.all_gather(owned_weight, 'dp', axis=0, tiled=True), p...]
    reduce_sum x1 -> x0, other arithmetic: 5.11 us -> none  [body(): mean_square = jnp.mean(widened * widened, axis=1, keepdims=True)]
  transfers between devices with their start and end apart: 3 -> 0, of which waited for: 3 -> 0; matrix products, arithmetic and copies ran while one was open for 1% -> 0% of each run, Pallas kernels for 0% -> 0%
where the time goes in v1:
time: 198 us; the launch traced here: 197 us
  Pallas kernels  193 us (97%)
  local copies, waits for them, and re-layouts  3.71 us (2%)
    pallas_call x1, Pallas kernels, body(): pl.pallas_call(block_kernel, name='prefill', out_shape=jax.ShapeDtypeStru...  134 us
    pallas_call x1, Pallas kernels, body(): pl.pallas_call(grad_kernel, name='grad_adam', out_shape=(jax.ShapeDtypeSt...  58.8 us

profile of v1, /device:TPU:0, one launch (start us, length us, event | category | flops | bytes accessed | tf_op | source)
XLA Modules:
  0.0 197.4 jit_solution(747193675964562265)
XLA Ops:
  0.6 58.8 %grad_adam.1 = (f32[512,768]{1,0:T(8,128)}, bf16[512,768]{1,0:T(8,128)(2,1)}) custom-call(bf16[256,8192]{1,0:T(8,128)(2,1)} %s_ref.1, bf16[256,768]{1,0:T(8,128)(2,1)} %c_ref.1, f32[512,768]{1,0:T(8,128)} %w_ref.1, f32[512,768]{1,0:T(8,128)} %m1_ref.1, f32[512,768]{1,0:T(8,128)} %m2_ref.1), custom_call_target="tpu_custom_call" | custom-call | tf_op jit(solution)/shard_map/grad_adam/pallas_call | solution.py:544
  59.4 134.2 %prefill.1 = bf16[64,8192]{1,0:T(8,128)(2,1)} custom-call(bf16[512,768]{1,0:T(8,128)(2,1)} %get-tuple-element.5.new_ref, bf16[512,8192]{1,0:T(8,128)(2,1)} %x_ref.1, f32[1,8192]{1,0:T(1,128)} %bitcast.1, bf16[512,8192]{1,0:T(8,128)(2,1)} %wo_ref.1, f32[512,128]{1,0:T(8,128)} %constant.4.clone.cos_ref, f32[512,128]{1,0:T(8,128)} %constant.5.clone.sin_ref), custom_call_target="tpu_custom_call" | custom-call | tf_op jit(solution)/shard_map/prefill/pallas_call | solution.py:569
  193.6 0.0 copy-start
  193.7 2.7 %copy.14 = f32[512,768]{1,0:T(8,128)} copy(f32[512,768]{1,0:T(8,128)} %get-tuple-element.8) | data formatting | bytes 3145728
  196.4 0.0 copy-done
  196.4 1.0 copy.15
Async XLA Ops:
  193.6 2.8 %copy-start = (bf16[64,8192]{1,0:T(8,128)(2,1)S(1)}, bf16[64,8192]{1,0:T(8,128)(2,1)}, u32[]{:S(2)}) copy-start(bf16[64,8192]{1,0:T(8,128)(2,1)} %prefill.1) | copy-start | bytes 3145732

commit v2 on v1

--- a/solution.py
+++ b/solution.py
@@ -1,5 +1,3 @@
-import functools
-
 import jax
 import jax.numpy as jnp
 import numpy as np
@@ -22,6 +20,9 @@
 HALF = D // 2
 CHUNKS = 4
 CW = HALF // CHUNKS
+HR = ROWS // 2
+NR = 32
+N_COPIES = 200
 
 beta_one = 0.9
 beta_two = 0.95
@@ -93,10 +94,10 @@
         dst = self.piece(rr, plane, lo, hi)
         if src is None:
             src = dst
-        self.cps.start(self.tag + name, src, dst, peer)
+        self.cps.start(self.tag + (name,), src, dst, peer)
 
     def wait(self, *names):
-        self.cps.arrived(*[self.tag + name for name in names])
+        self.cps.arrived(*[self.tag + (name,) for name in names])
 
     def begin(self, own=None):
         rows, cross = self.rows, self.cross
@@ -190,119 +191,31 @@
     return lax.rem(x + 4, 4) * 2 + yl
 
 
-def grad_kernel(
-    s_ref, c_ref, w_ref, m1_ref, m2_ref, upd_ref, new_ref,
-    sb, cb, g, wv, m1v, m2v, send, recv, local,
-):
-    d, t, z, yh, c, x, yl = place()
-    core = (d + 1 - 2 * c, t)
-    yhp = (dp_of(z, 1 - yh, c), t)
-    ylp = (d, t_of(x, 1 - yl))
-    xn, xp = (d, t_of(x + 1, yl)), (d, t_of(x - 1, yl))
-    zn, zp = (dp_of(z + 1, yh, c), t), (dp_of(z - 1, yh, c), t)
-    others = [lax.rem(d + j, N_DP) for j in range(1, N_DP)]
-
-    loads = [
-        pltpu.make_async_copy(c_ref, cb.at[d], local.at[0]),
-        pltpu.make_async_copy(
-            s_ref.at[pl.ds(mo(t * SUB, SUB), SUB), pl.ds(mo(d * ROWS, ROWS), ROWS)],
-            sb.at[t, pl.ds(mo(d * SUB, SUB), SUB), :],
-            local.at[1],
-        ),
-        pltpu.make_async_copy(w_ref, wv, local.at[2]),
-        pltpu.make_async_copy(m1_ref, m1v, local.at[3]),
-        pltpu.make_async_copy(m2_ref, m2v, local.at[4]),
-    ]
-    for cp in loads:
-        cp.start()
-    greet([(e, t) for e in others] + [xn, xp, ylp])
-
-    cps = Copies(send, recv)
-    for j, e in enumerate(others):
-        cps.start(
-            ("a", j),
-            s_ref.at[pl.ds(mo(t * SUB, SUB), SUB), pl.ds(mo(e * ROWS, ROWS), ROWS)],
-            sb.at[t, pl.ds(mo(d * SUB, SUB), SUB), :],
-            (e, t),
-        )
-    cot = Gather(
-        "c", cps, cb, lambda rr, p: dp_of(z + rr, yh + p * (1 - 2 * yh), c),
-        TOK, CROSS_C, zn, zp, yhp, core,
-    )
-    sta = Gather(
-        "s", cps, sb, lambda rr, p: t_of(x + rr, yl + p * (1 - 2 * yl)),
-        N_DP * SUB, CROSS_S, xn, xp, ylp,
-    )
-    cot.begin(c_ref)
-    cps.arrived(*[("a", j) for j in range(N_DP - 1)])
-    loads[1].wait()
-    sta.begin()
-    cot.step1()
-    cot.step2()
-    sta.step1()
-    cot.step3()
-    sta.step2()
-    cot.step4()
-    cot.step5()
-    sta.step3()
-    sta.step4()
-    cot.step6()
-    cot.step7()
-    sta.step5()
-    loads[0].wait()
-    cps.arrived(*["c" + n for n in ("c00", "c01", "c-0", "c+0", "c20", "c-1", "c+1", "c21")])
-
-    def term(tb):
-        cc = cb[:, pl.ds(mo(tb * SUB, SUB), SUB), :].reshape(N_DP * SUB, SLICE)
-        return lax.dot_general(
-            sb[tb], cc, (((0,), (0,)), ((), ())), preferred_element_type=F32
-        )
-
-    g[...] = term(t)
-
-    def ring(plane):
-        def one(i, carry):
-            g[...] += term(sta.index(i, plane))
-            return carry
-
-        return one
-
-    lax.fori_loop(1, 4, ring(0), 0)
-    g[...] += term(sta.index(0, 1))
-    sta.step6()
-    sta.step7()
-    lax.fori_loop(1, 4, ring(1), 0)
-    for cp in loads[2:]:
-        cp.wait()
-
-    def adam(i, carry):
-        r = pl.ds(mo(i * 32, 32), 32)
-        grad = g[r, :]
-        moment = beta_one * m1v[r, :] + (1.0 - beta_one) * grad
-        second = beta_two * m2v[r, :] + (1.0 - beta_two) * grad * grad
-        upd = moment / bias_one / (jnp.sqrt(second / bias_two) + adam_eps)
-        upd_ref[r, :] = upd
-        new_ref[r, :] = (wv[r, :] - learn_rate * upd).astype(BF)
-        return carry
-
-    lax.fori_loop(0, ROWS // 32, adam, 0)
-    cps.drain()
-
-
-def block_kernel(
-    new_ref, x_ref, gain_ref, wo_ref, cos_ref, sin_ref, out_ref,
-    wb, nb, stage, acc, kv, att, woo, wop, part, r1, r2, fp,
+def kernel(
+    s_ref, c_ref, w_ref, m1_ref, m2_ref, x_ref, gain_ref, wo_ref, cos_ref, sin_ref,
+    upd_ref, out_ref,
+    sb, cb, wv, m1v, m2v, wb, nb, stage, acc, kv, att, woo, wop, part, r1, r2, fp,
     send, recv, send2, recv2, local,
 ):
     d, t, z, yh, c, x, yl = place()
     core = (d + 1 - 2 * c, t)
     yhp = (dp_of(z, 1 - yh, c), t)
     ylp = (d, t_of(x, 1 - yl))
+    far_y = lax.rem(2 * yh + yl + 3 + 2 * yl, 4)
+    yfar = (dp_of(z, far_y // 2, c), t_of(x, lax.rem(far_y, 2)))
     xn, xp = (d, t_of(x + 1, yl)), (d, t_of(x - 1, yl))
     zn, zp = (dp_of(z + 1, yh, c), t), (dp_of(z - 1, yh, c), t)
+    others = [lax.rem(d + j, N_DP) for j in range(1, N_DP)]
     mine = mo(yl * HALF, HALF)
     theirs = mo((1 - yl) * HALF, HALF)
-    NR = 64
+
+    def spread(h, e):
+        return s_ref.at[
+            pl.ds(mo(t * SUB, SUB), SUB), pl.ds(mo(e * ROWS + h * HR, HR), HR)
+        ]
+
+    def landing(h):
+        return sb.at[h, t, pl.ds(mo(d * SUB, SUB), SUB), :]
 
     def fetch(i):
         return pltpu.make_async_copy(
@@ -310,20 +223,39 @@
             local.at[lax.rem(i, 2)],
         )
 
-    own = pltpu.make_async_copy(new_ref, wb.at[d], local.at[2])
-    out_w = pltpu.make_async_copy(wo_ref.at[:, pl.ds(mine, HALF)], woo, local.at[3])
+    own_c = pltpu.make_async_copy(c_ref, cb.at[d], local.at[2])
+    own_s = [pltpu.make_async_copy(spread(h, d), landing(h), local.at[3 + h]) for h in range(2)]
+    state = [
+        pltpu.make_async_copy(src, dst, local.at[5 + i])
+        for i, (src, dst) in enumerate(((w_ref, wv), (m1_ref, m1v), (m2_ref, m2v)))
+    ]
+    out_w = pltpu.make_async_copy(wo_ref.at[:, pl.ds(mine, HALF)], woo, local.at[8])
+    own_c.start()
+    for cp in own_s:
+        cp.start()
     fetch(0).start()
-    own.start()
-    greet([core, yhp, ylp, xn, xp, zn, zp])
+    greet([(e, t) for e in others] + [xn, xp, ylp, yfar])
 
     cps = Copies(send, recv)
-    gat = Gather(
-        "w", cps, wb, lambda rr, p: dp_of(z + rr, yh + p * (1 - 2 * yh), c),
-        ROWS, CROSS_W, zn, zp, yhp, core,
-    )
-    gat.begin(new_ref)
-    wrows = pl.ds(mo(c * (QW // 2), QW // 2), QW // 2)
-    cps.start("wo", wo_ref.at[wrows, pl.ds(theirs, HALF)], wop.at[wrows, :], ylp)
+    for h in range(2):
+        for j, e in enumerate(others):
+            cps.start(("a", h, j), spread(h, e), landing(h), (e, t))
+
+    def dp_index(rr, p):
+        return dp_of(z + rr, yh + p * (1 - 2 * yh), c)
+
+    def t_index(rr, p):
+        return t_of(x + rr, yl + p * (1 - 2 * yl))
+
+    cot = Gather(("c",), cps, cb, dp_index, TOK, CROSS_C, zn, zp, yhp, core)
+    sta = [
+        Gather(("s", h), cps, sb.at[h], t_index, N_DP * SUB, CROSS_S, xn, xp, ylp)
+        for h in range(2)
+    ]
+    gat = [
+        Gather(("w", h), cps, wb.at[h], dp_index, HR, CROSS_W, zn, zp, yhp, core)
+        for h in range(2)
+    ]
 
     def norm(i, carry):
         @pl.when(i + 1 < LEN // NR)
@@ -350,84 +282,167 @@
         lax.fori_loop(0, NR // 16, rows16, 0)
         return carry
 
-    lax.fori_loop(0, LEN // NR, norm, 0)
+    def term(h, tb):
+        cc = cb[:, pl.ds(mo(tb * SUB, SUB), SUB), :].reshape(N_DP * SUB, SLICE)
+        return lax.dot_general(
+            sb[h, tb], cc, (((0,), (0,)), ((), ())), preferred_element_type=F32
+        )
+
+    def gradient(h):
+        rows = pl.ds(h * HR, HR)
+        upd_ref[rows, :] = term(h, t)
+
+        def one(i, carry):
+            upd_ref[rows, :] += term(h, t_of(x + i // 2, lax.rem(yl + i, 2)))
+            return carry
+
+        lax.fori_loop(1, N_T, one, 0)
+
+        def adam(i, carry):
+            r = pl.ds(mo(h * HR + i * 32, 32), 32)
+            grad = upd_ref[r, :]
+            moment = beta_one * m1v[r, :] + (1.0 - beta_one) * grad
+            second = beta_two * m2v[r, :] + (1.0 - beta_two) * grad * grad
+            upd = moment / bias_one / (jnp.sqrt(second / bias_two) + adam_eps)
+            upd_ref[r, :] = upd
+            wb[h, d, pl.ds(mo(i * 32, 32), 32), :] = (wv[r, :] - learn_rate * upd).astype(BF)
+            return carry
+
+        lax.fori_loop(0, HR // 32, adam, 0)
+
+    def project(h, rr, plane):
+        e = dp_of(z + rr, yh + plane * (1 - 2 * yh), 0)
+        hc = slice(h * HR, (h + 1) * HR)
+        return jnp.dot(nb[e, :, hc], wb[h, e], preferred_element_type=F32) + jnp.dot(
+            nb[e + 1, :, hc], wb[h, e + 1], preferred_element_type=F32
+        )
+
+    def project_ring(h, plane):
+        def one(i, carry):
+            acc[...] += project(h, i, plane)
+            return carry
+
+        lax.fori_loop(1, 4, one, 0)
+
+    def here(h, *names):
+        cps.arrived(*[("w", h) + (n,) for n in names])
+
+    NN = LEN // NR
+    for h in range(2):
+        cps.arrived(*[("a", h, j) for j in range(N_DP - 1)])
+        own_s[h].wait()
+        if h == 0:
+            sta[0].begin()
+            cot.begin(c_ref)
+            for cp in state:
+                cp.start()
+    lax.fori_loop(0, 1, norm, 0)
+    sta[0].step1()
+    cot.step1()
+    cot.step2()
+    sta[0].step2()
+    wq = [pl.ds(mo((2 * c + i) * (QW // 4), QW // 4), QW // 4) for i in range(2)]
+    for i, peer in enumerate((ylp, yfar)):
+        cps.start(("o", i), wo_ref.at[wq[i], pl.ds(theirs, HALF)], wop.at[wq[i], :], peer)
+    lax.fori_loop(1, 3, norm, 0)
+    sta[0].step3()
+    cot.step3()
+    sta[0].step4()
+    sta[0].step5()
+    sta[1].begin()
+    cot.step4()
+    cot.step5()
+    lax.fori_loop(3, 6, norm, 0)
+    sta[0].step6()
+    sta[0].step7()
+    sta[1].step1()
+    cot.step6()
+    sta[1].step2()
+    lax.fori_loop(6, NN, norm, 0)
+    cot.step7()
+    own_c.wait()
+    for cp in state:
+        cp.wait()
+    cps.arrived(*[("c", n) for n in ("c00", "c01", "c-0", "c+0", "c20", "c-1", "c+1", "c21")])
+    gradient(0)
+    gat[0].begin()
+    sta[1].step3()
+    sta[1].step4()
+    sta[1].step5()
     out_w.start()
-
-    def term(e):
-        return jnp.dot(nb[e], wb[e], preferred_element_type=F32)
-
-    def pair(rr, plane):
-        base = dp_of(z + rr, yh + plane * (1 - 2 * yh), 0)
-
-        def one(i, carry):
-            acc[...] += term(base + i)
-            return carry
-
-        lax.fori_loop(0, 2, one, 0)
-
-    own.wait()
-    gat.step1()
-    gat.step2()
-    acc[...] = term(d)
-    cps.arrived("wc00")
-    acc[...] += term(d + 1 - 2 * c)
-    gat.step3()
-    gat.step4()
-    cps.arrived("wc01")
-    pair(0, 1)
-    gat.step5()
-    cps.arrived("wc-0", "wc+0", "wc20")
-
-    def ring(plane):
-        def one(i, carry):
-            e = dp_of(z + 1 + i // 2, yh + plane * (1 - 2 * yh), lax.rem(i, 2))
-            acc[...] += term(e)
-            return carry
-
-        lax.fori_loop(0, 6, one, 0)
-
-    ring(0)
-    cps.arrived("wo")
-    cps.start("woc", wop.at[wrows, :], wop.at[wrows, :], core)
-    gat.step6()
-    gat.step7()
-    cps.arrived("wc-1", "wc+1", "wc21")
-    ring(1)
-
-    def rope(u):
-        return u * cos_ref[...] + pltpu.roll(u, HD // 2, 1) * sin_ref[...]
-
-    kv[0] = rope(acc[:, QW : QW + HD]).astype(BF)
-    kv[1] = acc[:, QW + HD :].astype(BF)
-    HL = LEN // 2
-    for h in range(QH):
-        cols = slice(h * HD, (h + 1) * HD)
-        q = (rope(acc[:, cols]) * (HD**-0.5)).astype(BF)
-        for b in range(2):
-            n = HL * (b + 1)
-            s = lax.dot_general(
-                q[b * HL : n], kv[0, :n], (((1,), (1,)), ((), ())),
-                preferred_element_type=F32,
-            )
-            qi = lax.broadcasted_iota(jnp.int32, (HL, n), 0) + b * HL
-            ki = lax.broadcasted_iota(jnp.int32, (HL, n), 1)
-            s = jnp.where(qi >= ki, s, -jnp.inf)
-            e = jnp.exp(s - jnp.max(s, axis=1, keepdims=True))
-            a = (e / jnp.sum(e, axis=1, keepdims=True)).astype(BF)
-            att[0, b * HL : n, cols] = jnp.dot(
-                a, kv[1, :n], preferred_element_type=F32
-            ).astype(BF)
-        cps.start(("at", h), att.at[0, :, cols], att.at[1, :, cols], ylp)
-
-    out_w.wait()
-    cps.arrived("woc")
-    cps.arrived(*[("at", h) for h in range(QH)])
+    gat[0].step1()
+    here(0, "c00")
+    acc[...] = project(0, 0, 0)
+    gat[0].step2()
+    sta[1].step6()
+    gat[0].step3()
+    sta[1].step7()
+    gradient(1)
+    gat[0].step4()
+    gat[0].step5()
+    gat[1].begin()
+    here(0, "c01")
+    acc[...] += project(0, 0, 1)
+    here(0, "c-0", "c+0", "c20")
+    project_ring(0, 0)
+    gat[0].step6()
+    gat[1].step1()
+    gat[1].step2()
+    gat[0].step7()
+    here(1, "c00", "c01")
+    acc[...] += project(1, 0, 0)
+    here(0, "c-1", "c+1", "c21")
+    project_ring(0, 1)
+    gat[1].step3()
+    gat[1].step4()
+    acc[...] += project(1, 0, 1)
+    gat[1].step5()
+    cps.arrived(("o", 0), ("o", 1))
+    wc = pl.ds(mo(c * (QW // 2), QW // 2), QW // 2)
+    cps.start("oc", wop.at[wc, :], wop.at[wc, :], core)
+    here(1, "c-0", "c+0", "c20")
+    project_ring(1, 0)
+    gat[1].step6()
+    gat[1].step7()
+    here(1, "c-1", "c+1", "c21")
+    project_ring(1, 1)
+
+    def rope(u, rows):
+        return u * cos_ref[rows, :] + pltpu.roll(u, HD // 2, 1) * sin_ref[rows, :]
 
     XB = LEN // 4
     HC = CW // 2
+    whole = pl.ds(0, LEN)
+    kv[0] = rope(acc[:, QW : QW + HD], whole).astype(BF)
+    kv[1] = acc[:, QW + HD :].astype(BF)
 
     def rows_of(xx):
         return pl.ds(mo(lax.rem(xx + 4, 4) * XB, XB), XB)
+
+    def attend(xx):
+        rows = rows_of(xx)
+        q = jnp.concatenate(
+            [
+                (rope(acc[rows, h * HD : (h + 1) * HD], rows) * (HD**-0.5)).astype(BF)
+                for h in range(QH)
+            ],
+            axis=0,
+        )
+        s = lax.dot_general(
+            q, kv[0], (((1,), (1,)), ((), ())), preferred_element_type=F32
+        )
+        qi = lax.broadcasted_iota(jnp.int32, (QH * XB, LEN), 0) % XB
+        ki = lax.broadcasted_iota(jnp.int32, (QH * XB, LEN), 1)
+        s = jnp.where(qi + lax.rem(xx + 4, 4) * XB >= ki, s, -jnp.inf)
+        e = jnp.exp(s - jnp.max(s, axis=1, keepdims=True))
+        a = (e * (1.0 / jnp.sum(e, axis=1, keepdims=True))).astype(BF)
+        o = jnp.dot(a, kv[1], preferred_element_type=F32).astype(BF)
+        for h in range(QH):
+            att[0, rows, h * HD : (h + 1) * HD] = o[h * XB : (h + 1) * XB]
+
+    def share(i, xx):
+        rows = rows_of(xx)
+        cps.start(("t", i), att.at[0, rows, :], att.at[1, rows, :], ylp)
 
     def cols_of(k, w=CW, off=0):
         return pl.ds(mo(k * CW + off, HC), w)
@@ -455,19 +470,28 @@
         oc = pl.ds(mo(mine + k * CW, CW), CW)
         return remote(fp.at[:, cols_of(k)], out_ref.at[:, oc], 4 * CHUNKS + k, ylp)
 
-    def produce(k, carry):
-        def tile(j, carry):
-            cc = pl.ds(mo(k * CW + j * 256, 256), 256)
-            part[:, cc] = (
-                jnp.dot(att[0], woo[:, cc], preferred_element_type=F32)
-                + jnp.dot(att[1], wop[:, cc], preferred_element_type=F32)
-            ).astype(BF)
+    def produce(xx, then=None):
+        rows = rows_of(xx)
+
+        def chunk(k, carry):
+            def tile(j, carry):
+                cc = pl.ds(mo(k * CW + j * 256, 256), 256)
+                part[rows, cc] = (
+                    jnp.dot(att[0, rows, :], woo[:, cc], preferred_element_type=F32)
+                    + jnp.dot(att[1, rows, :], wop[:, cc], preferred_element_type=F32)
+                ).astype(BF)
+                return carry
+
+            lax.fori_loop(0, CW // 256, tile, 0)
+            if then is not None:
+                then(k)
             return carry
 
-        lax.fori_loop(0, CW // 256, tile, 0)
+        lax.fori_loop(0, CHUNKS, chunk, 0)
+
+    def send_far(k):
         for cp in far(k):
             cp.start()
-        return carry
 
     def forward(k, carry):
         hc = pl.ds(mo(k * HC, HC), HC)
@@ -511,8 +535,24 @@
         last(k).wait()
         return carry
 
-    lax.fori_loop(0, CHUNKS, produce, 0)
+    attend(x + 2)
+    share(0, x + 2)
+    attend(x + 1)
+    share(1, x + 1)
+    out_w.wait()
+    cps.arrived("oc", ("t", 0))
+    produce(x + 2, send_far)
+    attend(x - 1)
+    share(2, x - 1)
+    attend(x)
+    share(3, x)
+    cps.arrived(("t", 1))
+    produce(x + 1)
+    cps.arrived(("t", 2))
+    produce(x - 1)
     lax.fori_loop(0, CHUNKS, forward, 0)
+    cps.arrived(("t", 3))
+    produce(x)
     lax.fori_loop(0, CHUNKS, finish, 0)
     lax.fori_loop(0, CHUNKS, close, 0)
     cps.drain()
@@ -520,7 +560,7 @@
 
 CROSS_C = TOK
 CROSS_S = N_DP * SUB
-CROSS_W = ROWS
+CROSS_W = HR
 
 
 def tables():
@@ -537,45 +577,27 @@
 VM = pl.BlockSpec(memory_space=pltpu.VMEM)
 
 
-def body(
-    train_states, qkv_cotangent, w_master, moment_one, moment_two, prompt_states, norm_gain, w_out
-):
+def step(*args, name="adam_prefill"):
     dma = pltpu.SemaphoreType.DMA
-    update_dir, fresh = pl.pallas_call(
-        grad_kernel,
-        name="grad_adam",
+    cos, sin = tables()
+    return pl.pallas_call(
+        kernel,
+        name=name,
         out_shape=(
             jax.ShapeDtypeStruct((ROWS, SLICE), F32),
-            jax.ShapeDtypeStruct((ROWS, SLICE), BF),
+            jax.ShapeDtypeStruct((LEN // N_T, D), BF),
         ),
-        in_specs=[ANY] * 5,
+        in_specs=[ANY] * 6 + [VM, ANY, VM, VM],
         out_specs=(VM, VM),
         scratch_shapes=[
-            pltpu.VMEM((N_T, N_DP * SUB, ROWS), BF),
+            pltpu.VMEM((2, N_T, N_DP * SUB, HR), BF),
             pltpu.VMEM((N_DP, TOK, SLICE), BF),
             pltpu.VMEM((ROWS, SLICE), F32),
             pltpu.VMEM((ROWS, SLICE), F32),
             pltpu.VMEM((ROWS, SLICE), F32),
-            pltpu.VMEM((ROWS, SLICE), F32),
-            dma((64,)),
-            dma((64,)),
-            dma((5,)),
-        ],
-        compiler_params=pltpu.CompilerParams(
-            collective_id=1, has_side_effects=True, vmem_limit_bytes=60 << 20
-        ),
-    )(train_states, qkv_cotangent, w_master, moment_one, moment_two)
-    cos, sin = tables()
-    out = pl.pallas_call(
-        block_kernel,
-        name="prefill",
-        out_shape=jax.ShapeDtypeStruct((LEN // N_T, D), BF),
-        in_specs=[ANY, ANY, VM, ANY, VM, VM],
-        out_specs=VM,
-        scratch_shapes=[
-            pltpu.VMEM((N_DP, ROWS, SLICE), BF),
+            pltpu.VMEM((2, N_DP, HR, SLICE), BF),
             pltpu.VMEM((N_DP, LEN, ROWS), BF),
-            pltpu.VMEM((2, 64, D), BF),
+            pltpu.VMEM((2, NR, D), BF),
             pltpu.VMEM((LEN, SLICE), F32),
             pltpu.VMEM((2, LEN, HD), BF),
             pltpu.VMEM((2, LEN, QW), BF),
@@ -585,17 +607,25 @@
             pltpu.VMEM((2, LEN // 4, HALF // 2), BF),
             pltpu.VMEM((2, LEN // 4, HALF), BF),
             pltpu.VMEM((LEN // N_T, HALF), BF),
-            dma((48,)),
-            dma((48,)),
+            dma((N_COPIES,)),
+            dma((N_COPIES,)),
             dma((5 * CHUNKS,)),
             dma((5 * CHUNKS,)),
-            dma((4,)),
+            dma((9,)),
         ],
         compiler_params=pltpu.CompilerParams(
-            collective_id=2, has_side_effects=True, vmem_limit_bytes=63 << 20
+            collective_id=1, has_side_effects=True, vmem_limit_bytes=67043328
         ),
-    )(fresh, prompt_states, norm_gain.reshape(1, D), w_out, jnp.asarray(cos), jnp.asarray(sin))
-    return (update_dir, out)
+    )(*args[:6], args[6].reshape(1, D), args[7], jnp.asarray(cos), jnp.asarray(sin))
+
+
+def body(
+    train_states, qkv_cotangent, w_master, moment_one, moment_two, prompt_states, norm_gain, w_out
+):
+    return step(
+        train_states, qkv_cotangent, w_master, moment_one, moment_two,
+        prompt_states, norm_gain, w_out,
+    )
 
 
 def solution(mesh):

time: 198 us -> 189 us (0.955)
  Pallas kernels: 193 us -> 184 us
    pallas_call x2 -> x1, Pallas kernels: 193 us -> 184 us  [step(): pl.pallas_call(kernel, name=name, out_shape=(jax.ShapeDtypeStruct((ROWS,...]
where the time goes in v2:
time: 189 us; the launch traced here: 188 us
  Pallas kernels  184 us (97%)
  local copies, waits for them, and re-layouts  3.71 us (2%)
    pallas_call x1, Pallas kernels, step(): pl.pallas_call(kernel, name=name, out_shape=(jax.ShapeDtypeStruct((ROWS,...  184 us

profile of v2, /device:TPU:0, one launch (start us, length us, event | category | flops | bytes accessed | tf_op | source)
XLA Modules:
  0.0 188.4 jit_solution(4469880790100011369)
XLA Ops:
  0.6 184.0 %adam_prefill.1 = (f32[512,768]{1,0:T(8,128)}, bf16[64,8192]{1,0:T(8,128)(2,1)}) custom-call(bf16[256,8192]{1,0:T(8,128)(2,1)} %s_ref.1, bf16[256,768]{1,0:T(8,128)(2,1)} %c_ref.1, f32[512,768]{1,0:T(8,128)} %w_ref.1, f32[512,768]{1,0:T(8,128)} %m1_ref.1, f32[512,768]{1,0:T(8,128)} %m2_ref.1, bf16[512,8192]{1,0:T(8,128)(2,1)} %x_ref.1, f32[1,8192]{1,0:T(1,128)} %bitcast.1, ...), custom_call_target="tpu_custom_call" | custom-call | tf_op jit(solution)/shard_map/adam_prefill/pallas_call | solution.py:583
  184.7 0.0 copy-start
  184.7 2.7 %copy.14 = f32[512,768]{1,0:T(8,128)} copy(f32[512,768]{1,0:T(8,128)} %get-tuple-element.4) | data formatting | bytes 3145728
  187.4 0.0 copy-done
  187.4 1.0 copy.15
Async XLA Ops:
  184.7 2.8 %copy-start = (bf16[64,8192]{1,0:T(8,128)(2,1)S(1)}, bf16[64,8192]{1,0:T(8,128)(2,1)}, u32[]{:S(2)}) copy-start(bf16[64,8192]{1,0:T(8,128)(2,1)} %get-tuple-element.5) | copy-start | bytes 3145732

commit v3 on v2

--- a/solution.py
+++ b/solution.py
@@ -82,13 +82,16 @@
 
 
 class Gather:
-    def __init__(self, tag, cps, buf, index, rows, cross, nxt, prv, partner, core=None):
+    def __init__(
+        self, tag, cps, buf, index, rows, cross, nxt, prv, partner, core=None, cols=None
+    ):
         self.tag, self.cps, self.buf, self.index = tag, cps, buf, index
         self.rows, self.cross = rows, cross
         self.nxt, self.prv, self.partner, self.core = nxt, prv, partner, core
+        self.cols = slice(None) if cols is None else pl.ds(*cols)
 
     def piece(self, rr, plane, lo, hi):
-        return self.buf.at[self.index(rr, plane), pl.ds(lo, hi - lo), :]
+        return self.buf.at[self.index(rr, plane), pl.ds(lo, hi - lo), self.cols]
 
     def go(self, name, rr, plane, lo, hi, peer, src=None):
         dst = self.piece(rr, plane, lo, hi)
@@ -194,7 +197,7 @@
 def kernel(
     s_ref, c_ref, w_ref, m1_ref, m2_ref, x_ref, gain_ref, wo_ref, cos_ref, sin_ref,
     upd_ref, out_ref,
-    sb, cb, wv, m1v, m2v, wb, nb, stage, acc, kv, att, woo, wop, part, r1, r2, fp,
+    sv, sb, cb, wv, m1v, m2v, wb, nb, stage, acc, kv, att, woo, wop, part, r1, r2, fp,
     send, recv, send2, recv2, local,
 ):
     d, t, z, yh, c, x, yl = place()
@@ -209,13 +212,10 @@
     mine = mo(yl * HALF, HALF)
     theirs = mo((1 - yl) * HALF, HALF)
 
-    def spread(h, e):
-        return s_ref.at[
-            pl.ds(mo(t * SUB, SUB), SUB), pl.ds(mo(e * ROWS + h * HR, HR), HR)
-        ]
-
-    def landing(h):
-        return sb.at[h, t, pl.ds(mo(d * SUB, SUB), SUB), :]
+    def spread(e):
+        return sv.at[:, pl.ds(mo(e * ROWS, ROWS), ROWS)]
+
+    landing = sb.at[t, pl.ds(mo(d * SUB, SUB), SUB), :]
 
     def fetch(i):
         return pltpu.make_async_copy(
@@ -224,22 +224,20 @@
         )
 
     own_c = pltpu.make_async_copy(c_ref, cb.at[d], local.at[2])
-    own_s = [pltpu.make_async_copy(spread(h, d), landing(h), local.at[3 + h]) for h in range(2)]
+    load_s = pltpu.make_async_copy(s_ref.at[pl.ds(mo(t * SUB, SUB), SUB), :], sv, local.at[3])
+    own_s = pltpu.make_async_copy(spread(d), landing, local.at[4])
     state = [
         pltpu.make_async_copy(src, dst, local.at[5 + i])
         for i, (src, dst) in enumerate(((w_ref, wv), (m1_ref, m1v), (m2_ref, m2v)))
     ]
     out_w = pltpu.make_async_copy(wo_ref.at[:, pl.ds(mine, HALF)], woo, local.at[8])
+    load_s.start()
     own_c.start()
-    for cp in own_s:
-        cp.start()
     fetch(0).start()
     greet([(e, t) for e in others] + [xn, xp, ylp, yfar])
+    load_s.wait()
 
     cps = Copies(send, recv)
-    for h in range(2):
-        for j, e in enumerate(others):
-            cps.start(("a", h, j), spread(h, e), landing(h), (e, t))
 
     def dp_index(rr, p):
         return dp_of(z + rr, yh + p * (1 - 2 * yh), c)
@@ -249,7 +247,7 @@
 
     cot = Gather(("c",), cps, cb, dp_index, TOK, CROSS_C, zn, zp, yhp, core)
     sta = [
-        Gather(("s", h), cps, sb.at[h], t_index, N_DP * SUB, CROSS_S, xn, xp, ylp)
+        Gather(("s", h), cps, sb, t_index, N_DP * SUB, CROSS_S, xn, xp, ylp, None, (h * HR, HR))
         for h in range(2)
     ]
     gat = [
@@ -285,7 +283,7 @@
     def term(h, tb):
         cc = cb[:, pl.ds(mo(tb * SUB, SUB), SUB), :].reshape(N_DP * SUB, SLICE)
         return lax.dot_general(
-            sb[h, tb], cc, (((0,), (0,)), ((), ())), preferred_element_type=F32
+            sb[tb, :, h * HR : (h + 1) * HR], cc, (((0,), (0,)), ((), ())), preferred_element_type=F32
         )
 
     def gradient(h):
@@ -328,81 +326,80 @@
         cps.arrived(*[("w", h) + (n,) for n in names])
 
     NN = LEN // NR
-    for h in range(2):
-        cps.arrived(*[("a", h, j) for j in range(N_DP - 1)])
-        own_s[h].wait()
-        if h == 0:
-            sta[0].begin()
-            cot.begin(c_ref)
-            for cp in state:
-                cp.start()
-    lax.fori_loop(0, 1, norm, 0)
+    for j, e in enumerate(others):
+        cps.start(("a", j), spread(e), landing, (e, t))
+    own_s.start()
+    cot.begin(c_ref)
+    for cp in state:
+        cp.start()
+    lax.fori_loop(0, 7, norm, 0)
+    cps.arrived(*[("a", j) for j in range(N_DP - 1)])
+    own_s.wait()
+    sta[0].begin()
+    cot.step1()
     sta[0].step1()
-    cot.step1()
     cot.step2()
     sta[0].step2()
-    wq = [pl.ds(mo((2 * c + i) * (QW // 4), QW // 4), QW // 4) for i in range(2)]
-    for i, peer in enumerate((ylp, yfar)):
-        cps.start(("o", i), wo_ref.at[wq[i], pl.ds(theirs, HALF)], wop.at[wq[i], :], peer)
-    lax.fori_loop(1, 3, norm, 0)
     sta[0].step3()
     cot.step3()
     sta[0].step4()
+    cot.step4()
     sta[0].step5()
     sta[1].begin()
-    cot.step4()
     cot.step5()
-    lax.fori_loop(3, 6, norm, 0)
+    lax.fori_loop(7, NN, norm, 0)
     sta[0].step6()
+    cot.step6()
+    cot.step7()
     sta[0].step7()
-    sta[1].step1()
-    cot.step6()
-    sta[1].step2()
-    lax.fori_loop(6, NN, norm, 0)
-    cot.step7()
     own_c.wait()
     for cp in state:
         cp.wait()
     cps.arrived(*[("c", n) for n in ("c00", "c01", "c-0", "c+0", "c20", "c-1", "c+1", "c21")])
     gradient(0)
     gat[0].begin()
+    wq = [pl.ds(mo((2 * c + i) * (QW // 4), QW // 4), QW // 4) for i in range(2)]
+    for i, peer in enumerate((ylp, yfar)):
+        cps.start(("o", i), wo_ref.at[wq[i], pl.ds(theirs, HALF)], wop.at[wq[i], :], peer)
+    sta[1].step1()
+    sta[1].step2()
+    out_w.start()
+    gat[0].step1()
+    gat[0].step2()
     sta[1].step3()
     sta[1].step4()
+    gat[0].step3()
     sta[1].step5()
-    out_w.start()
-    gat[0].step1()
     here(0, "c00")
     acc[...] = project(0, 0, 0)
-    gat[0].step2()
+    gat[0].step4()
     sta[1].step6()
-    gat[0].step3()
+    gat[0].step5()
     sta[1].step7()
     gradient(1)
-    gat[0].step4()
-    gat[0].step5()
     gat[1].begin()
     here(0, "c01")
     acc[...] += project(0, 0, 1)
     here(0, "c-0", "c+0", "c20")
     project_ring(0, 0)
     gat[0].step6()
+    gat[0].step7()
     gat[1].step1()
     gat[1].step2()
-    gat[0].step7()
-    here(1, "c00", "c01")
-    acc[...] += project(1, 0, 0)
     here(0, "c-1", "c+1", "c21")
     project_ring(0, 1)
     gat[1].step3()
+    here(1, "c00", "c01")
+    acc[...] += project(1, 0, 0)
     gat[1].step4()
     acc[...] += project(1, 0, 1)
     gat[1].step5()
     cps.arrived(("o", 0), ("o", 1))
     wc = pl.ds(mo(c * (QW // 2), QW // 2), QW // 2)
     cps.start("oc", wop.at[wc, :], wop.at[wc, :], core)
+    gat[1].step6()
     here(1, "c-0", "c+0", "c20")
     project_ring(1, 0)
-    gat[1].step6()
     gat[1].step7()
     here(1, "c-1", "c+1", "c21")
     project_ring(1, 1)
@@ -558,9 +555,9 @@
     cps.drain()
 
 
-CROSS_C = TOK
+CROSS_C = 160
 CROSS_S = N_DP * SUB
-CROSS_W = HR
+CROSS_W = 224
 
 
 def tables():
@@ -590,7 +587,8 @@
         in_specs=[ANY] * 6 + [VM, ANY, VM, VM],
         out_specs=(VM, VM),
         scratch_shapes=[
-            pltpu.VMEM((2, N_T, N_DP * SUB, HR), BF),
+            pltpu.VMEM((SUB, D), BF),
+            pltpu.VMEM((N_T, N_DP * SUB, ROWS), BF),
             pltpu.VMEM((N_DP, TOK, SLICE), BF),
             pltpu.VMEM((ROWS, SLICE), F32),
             pltpu.VMEM((ROWS, SLICE), F32),

time: 189 us -> 166 us (0.88)
  Pallas kernels: 184 us -> 161 us
    pallas_call x1, Pallas kernels: 184 us -> 161 us  [step(): pl.pallas_call(kernel, name=name, out_shape=(jax.ShapeDtypeStruct((ROWS,...]
where the time goes in v3:
time: 166 us
  Pallas kernels  161 us (97%)
  local copies, waits for them, and re-layouts  3.71 us (2%)
    pallas_call x1, Pallas kernels, step(): pl.pallas_call(kernel, name=name, out_shape=(jax.ShapeDtypeStruct((ROWS,...  161 us
    unnamed x4, local copies, waits for them, and re-layouts  3.71 us

profile of v3, /device:TPU:0, one launch (start us, length us, event | category | flops | bytes accessed | tf_op | source)
XLA Modules:
  0.0 165.7 jit_solution(9454141394867518628)
XLA Ops:
  0.6 161.4 %adam_prefill.1 = (f32[512,768]{1,0:T(8,128)}, bf16[64,8192]{1,0:T(8,128)(2,1)}) custom-call(bf16[256,8192]{1,0:T(8,128)(2,1)} %s_ref.1, bf16[256,768]{1,0:T(8,128)(2,1)} %c_ref.1, f32[512,768]{1,0:T(8,128)} %w_ref.1, f32[512,768]{1,0:T(8,128)} %m1_ref.1, f32[512,768]{1,0:T(8,128)} %m2_ref.1, bf16[512,8192]{1,0:T(8,128)(2,1)} %x_ref.1, f32[1,8192]{1,0:T(1,128)} %bitcast.1, ...), custom_call_target="tpu_custom_call" | custom-call | tf_op jit(solution)/shard_map/adam_prefill/pallas_call | solution.py:580
  162.0 0.0 copy-start
  162.0 2.7 %copy.14 = f32[512,768]{1,0:T(8,128)} copy(f32[512,768]{1,0:T(8,128)} %get-tuple-element.4) | data formatting | bytes 3145728
  164.7 0.0 copy-done
  164.7 1.0 copy.15
Async XLA Ops:
  162.0 2.8 %copy-start = (bf16[64,8192]{1,0:T(8,128)(2,1)S(1)}, bf16[64,8192]{1,0:T(8,128)(2,1)}, u32[]{:S(2)}) copy-start(bf16[64,8192]{1,0:T(8,128)(2,1)} %get-tuple-element.5) | copy-start | bytes 3145732

commit v4 on v3

--- a/solution.py
+++ b/solution.py
@@ -83,15 +83,14 @@
 
 class Gather:
     def __init__(
-        self, tag, cps, buf, index, rows, cross, nxt, prv, partner, core=None, cols=None
+        self, tag, cps, buf, index, rows, cross, nxt, prv, partner, core=None
     ):
         self.tag, self.cps, self.buf, self.index = tag, cps, buf, index
         self.rows, self.cross = rows, cross
         self.nxt, self.prv, self.partner, self.core = nxt, prv, partner, core
-        self.cols = slice(None) if cols is None else pl.ds(*cols)
 
     def piece(self, rr, plane, lo, hi):
-        return self.buf.at[self.index(rr, plane), pl.ds(lo, hi - lo), self.cols]
+        return self.buf.at[self.index(rr, plane), pl.ds(lo, hi - lo), :]
 
     def go(self, name, rr, plane, lo, hi, peer, src=None):
         dst = self.piece(rr, plane, lo, hi)
@@ -197,7 +196,7 @@
 def kernel(
     s_ref, c_ref, w_ref, m1_ref, m2_ref, x_ref, gain_ref, wo_ref, cos_ref, sin_ref,
     upd_ref, out_ref,
-    sv, sb, cb, wv, m1v, m2v, wb, nb, stage, acc, kv, att, woo, wop, part, r1, r2, fp,
+    sv, ld, sb, cb, wv, m1v, m2v, wb, nb, stage, acc, kv, att, woo, wop, part, r1, r2, fp,
     send, recv, send2, recv2, local,
 ):
     d, t, z, yh, c, x, yl = place()
@@ -215,7 +214,7 @@
     def spread(e):
         return sv.at[:, pl.ds(mo(e * ROWS, ROWS), ROWS)]
 
-    landing = sb.at[t, pl.ds(mo(d * SUB, SUB), SUB), :]
+    landing = ld.at[pl.ds(mo(d * SUB, SUB), SUB), :]
 
     def fetch(i):
         return pltpu.make_async_copy(
@@ -231,6 +230,10 @@
         for i, (src, dst) in enumerate(((w_ref, wv), (m1_ref, m1v), (m2_ref, m2v)))
     ]
     out_w = pltpu.make_async_copy(wo_ref.at[:, pl.ds(mine, HALF)], woo, local.at[8])
+    split = [
+        pltpu.make_async_copy(ld.at[:, pl.ds(h * HR, HR)], sb.at[h, t], local.at[9 + h])
+        for h in range(2)
+    ]
     load_s.start()
     own_c.start()
     fetch(0).start()
@@ -247,7 +250,7 @@
 
     cot = Gather(("c",), cps, cb, dp_index, TOK, CROSS_C, zn, zp, yhp, core)
     sta = [
-        Gather(("s", h), cps, sb, t_index, N_DP * SUB, CROSS_S, xn, xp, ylp, None, (h * HR, HR))
+        Gather(("s", h), cps, sb.at[h], t_index, N_DP * SUB, CROSS_S, xn, xp, ylp)
         for h in range(2)
     ]
     gat = [
@@ -283,7 +286,7 @@
     def term(h, tb):
         cc = cb[:, pl.ds(mo(tb * SUB, SUB), SUB), :].reshape(N_DP * SUB, SLICE)
         return lax.dot_general(
-            sb[tb, :, h * HR : (h + 1) * HR], cc, (((0,), (0,)), ((), ())), preferred_element_type=F32
+            sb[h, tb], cc, (((0,), (0,)), ((), ())), preferred_element_type=F32
         )
 
     def gradient(h):
@@ -335,6 +338,9 @@
     lax.fori_loop(0, 7, norm, 0)
     cps.arrived(*[("a", j) for j in range(N_DP - 1)])
     own_s.wait()
+    for cp in split:
+        cp.start()
+    split[0].wait()
     sta[0].begin()
     cot.step1()
     sta[0].step1()
@@ -345,6 +351,7 @@
     sta[0].step4()
     cot.step4()
     sta[0].step5()
+    split[1].wait()
     sta[1].begin()
     cot.step5()
     lax.fori_loop(7, NN, norm, 0)
@@ -358,9 +365,14 @@
     cps.arrived(*[("c", n) for n in ("c00", "c01", "c-0", "c+0", "c20", "c-1", "c+1", "c21")])
     gradient(0)
     gat[0].begin()
-    wq = [pl.ds(mo((2 * c + i) * (QW // 4), QW // 4), QW // 4) for i in range(2)]
-    for i, peer in enumerate((ylp, yfar)):
-        cps.start(("o", i), wo_ref.at[wq[i], pl.ds(theirs, HALF)], wop.at[wq[i], :], peer)
+    NP = QW // 8
+
+    def weights(k):
+        for i, peer in enumerate((ylp, yfar)):
+            rows = pl.ds(mo((2 * c + i) * (QW // 4) + k * NP, NP), NP)
+            cps.start(("o", i, k), wo_ref.at[rows, pl.ds(theirs, HALF)], wop.at[rows, :], peer)
+
+    weights(0)
     sta[1].step1()
     sta[1].step2()
     out_w.start()
@@ -378,6 +390,7 @@
     sta[1].step7()
     gradient(1)
     gat[1].begin()
+    weights(1)
     here(0, "c01")
     acc[...] += project(0, 0, 1)
     here(0, "c-0", "c+0", "c20")
@@ -394,7 +407,7 @@
     gat[1].step4()
     acc[...] += project(1, 0, 1)
     gat[1].step5()
-    cps.arrived(("o", 0), ("o", 1))
+    cps.arrived(*[("o", i, k) for i in range(2) for k in range(2)])
     wc = pl.ds(mo(c * (QW // 2), QW // 2), QW // 2)
     cps.start("oc", wop.at[wc, :], wop.at[wc, :], core)
     gat[1].step6()
@@ -588,7 +601,8 @@
         out_specs=(VM, VM),
         scratch_shapes=[
             pltpu.VMEM((SUB, D), BF),
-            pltpu.VMEM((N_T, N_DP * SUB, ROWS), BF),
+            pltpu.VMEM((N_DP * SUB, ROWS), BF),
+            pltpu.VMEM((2, N_T, N_DP * SUB, HR), BF),
             pltpu.VMEM((N_DP, TOK, SLICE), BF),
             pltpu.VMEM((ROWS, SLICE), F32),
             pltpu.VMEM((ROWS, SLICE), F32),
@@ -609,7 +623,7 @@
             dma((N_COPIES,)),
             dma((5 * CHUNKS,)),
             dma((5 * CHUNKS,)),
-            dma((9,)),
+            dma((11,)),
         ],
         compiler_params=pltpu.CompilerParams(
             collective_id=1, has_side_effects=True, vmem_limit_bytes=67043328

time: 166 us -> 160 us (0.964)
  Pallas kernels: 161 us -> 156 us
    pallas_call x1, Pallas kernels: 161 us -> 156 us  [step(): pl.pallas_call(kernel, name=name, out_shape=(jax.ShapeDtypeStruct((ROWS,...]
where the time goes in v4:
time: 160 us
  Pallas kernels  156 us (98%)
  local copies, waits for them, and re-layouts  3.71 us (2%)
    pallas_call x1, Pallas kernels, step(): pl.pallas_call(kernel, name=name, out_shape=(jax.ShapeDtypeStruct((ROWS,...  156 us
    unnamed x4, local copies, waits for them, and re-layouts  3.71 us

profile of v4, /device:TPU:0, one launch (start us, length us, event | category | flops | bytes accessed | tf_op | source)
XLA Modules:
  0.0 160.0 jit_solution(1185135077347522879)
XLA Ops:
  0.6 155.6 %adam_prefill.1 = (f32[512,768]{1,0:T(8,128)}, bf16[64,8192]{1,0:T(8,128)(2,1)}) custom-call(bf16[256,8192]{1,0:T(8,128)(2,1)} %s_ref.1, bf16[256,768]{1,0:T(8,128)(2,1)} %c_ref.1, f32[512,768]{1,0:T(8,128)} %w_ref.1, f32[512,768]{1,0:T(8,128)} %m1_ref.1, f32[512,768]{1,0:T(8,128)} %m2_ref.1, bf16[512,8192]{1,0:T(8,128)(2,1)} %x_ref.1, f32[1,8192]{1,0:T(1,128)} %bitcast.1, ...), custom_call_target="tpu_custom_call" | custom-call | tf_op jit(solution)/shard_map/adam_prefill/pallas_call | solution.py:593
  156.3 0.0 copy-start
  156.3 2.7 %copy.14 = f32[512,768]{1,0:T(8,128)} copy(f32[512,768]{1,0:T(8,128)} %get-tuple-element.4) | data formatting | bytes 3145728
  159.0 0.0 copy-done
  159.0 1.0 copy.15
Async XLA Ops:
  156.3 2.8 %copy-start = (bf16[64,8192]{1,0:T(8,128)(2,1)S(1)}, bf16[64,8192]{1,0:T(8,128)(2,1)}, u32[]{:S(2)}) copy-start(bf16[64,8192]{1,0:T(8,128)(2,1)} %get-tuple-element.5) | copy-start | bytes 3145732

commit v5 on v4

--- a/solution.py
+++ b/solution.py
@@ -568,7 +568,7 @@
     cps.drain()
 
 
-CROSS_C = 160
+CROSS_C = 192
 CROSS_S = N_DP * SUB
 CROSS_W = 224
 
@@ -631,12 +631,40 @@
     )(*args[:6], args[6].reshape(1, D), args[7], jnp.asarray(cos), jnp.asarray(sin))
 
 
+def hand_over_kernel(u_ref, o_ref, u_out, o_out, sem):
+    cps = [
+        pltpu.make_async_copy(u_ref, u_out, sem.at[0]),
+        pltpu.make_async_copy(o_ref, o_out, sem.at[1]),
+    ]
+    for cp in cps:
+        cp.start()
+    for cp in cps:
+        cp.wait()
+
+
+def hand_over(upd, out):
+    return pl.pallas_call(
+        hand_over_kernel,
+        name="hand_over",
+        out_shape=(
+            jax.ShapeDtypeStruct(upd.shape, upd.dtype),
+            jax.ShapeDtypeStruct(out.shape, out.dtype),
+        ),
+        in_specs=[VM, VM],
+        out_specs=(ANY, ANY),
+        scratch_shapes=[pltpu.SemaphoreType.DMA((2,))],
+        compiler_params=pltpu.CompilerParams(vmem_limit_bytes=8 << 20),
+    )(upd, out)
+
+
 def body(
     train_states, qkv_cotangent, w_master, moment_one, moment_two, prompt_states, norm_gain, w_out
 ):
-    return step(
-        train_states, qkv_cotangent, w_master, moment_one, moment_two,
-        prompt_states, norm_gain, w_out,
+    return hand_over(
+        *step(
+            train_states, qkv_cotangent, w_master, moment_one, moment_two,
+            prompt_states, norm_gain, w_out,
+        )
     )
 
 

time: 160 us -> 159 us (level); the launches traced: 160 us -> 157 us
  Pallas kernels: 156 us -> 154 us
    pallas_call x1, Pallas kernels: 156 us -> 152 us  [step(): pl.pallas_call(kernel, name=name, out_shape=(jax.ShapeDtypeStruct((ROWS,...]
where the time goes in v5:
time: 159 us; the launch traced here: 157 us
  Pallas kernels  154 us (97%)
  local copies, waits for them, and re-layouts  2.63 us (2%)
    pallas_call x1, Pallas kernels, step(): pl.pallas_call(kernel, name=name, out_shape=(jax.ShapeDtypeStruct((ROWS,...  152 us

profile of v5, /device:TPU:0, one launch (start us, length us, event | category | flops | bytes accessed | tf_op | source)
XLA Modules:
  0.0 156.9 jit_solution(14614711549892616512)
XLA Ops:
  0.6 152.1 %adam_prefill.1 = (f32[512,768]{1,0:T(8,128)}, bf16[64,8192]{1,0:T(8,128)(2,1)}) custom-call(bf16[256,8192]{1,0:T(8,128)(2,1)} %s_ref.1, bf16[256,768]{1,0:T(8,128)(2,1)} %c_ref.1, f32[512,768]{1,0:T(8,128)} %w_ref.1, f32[512,768]{1,0:T(8,128)} %m1_ref.1, f32[512,768]{1,0:T(8,128)} %m2_ref.1, bf16[512,8192]{1,0:T(8,128)(2,1)} %x_ref.1, f32[1,8192]{1,0:T(1,128)} %bitcast.1, ...), custom_call_target="tpu_custom_call" | custom-call | tf_op jit(solution)/shard_map/adam_prefill/pallas_call | solution.py:593
  152.8 0.0 copy-start
  152.8 1.4 copy-done
  154.2 0.0 copy-start.1
  154.2 1.2 copy-done.1
  155.4 1.5 hand_over.1
Async XLA Ops:
  152.8 1.4 copy-start
  154.2 1.2 copy-start.1
